TPU v7x, 256 devices: a whole 4x4x8 slice. The times are simulated.
256 devices in a mesh: tm: 4 (over z_hi, core), height: 16 (over x, y), width: 4 (over z_lo).
Axes of the slice: x: 4, y: 4, z: 8 (z_hi: 2, z_lo: 4; z = z_hi * 4 + z_lo), core: 2. Of those that a mesh axis runs over, the one named last changes fastest.
Arguments:
- frames: bfloat16 [8, 64, 128, 384], P('tm', 'height', 'width'), may hold values from -6 to 6
- cache_in: bfloat16 [2, 64, 128, 384], P(None, 'height', 'width'), may hold values from -6 to 6
- kernel: bfloat16 [384, 3, 3, 3, 384], replicated, may hold values from -0.0625 to 0.0625
- conv_bias: float32 [384], replicated, may hold values from -3 to 3
- cotangent: bfloat16 [8, 64, 128, 384], P('tm', 'height', 'width'), may hold values from -6 to 6
Outputs:
- decoded: bfloat16 [8, 64, 128, 384], P('tm', 'height', 'width')
- frame_grad: bfloat16 [8, 64, 128, 384], P('tm', 'height', 'width')
- cache_grad: bfloat16 [8, 64, 128, 384], P('tm', 'height', 'width')
- kernel_grad: float32 [384, 3, 3, 3, 384], P('height')
All inputs are finite; a program needn't handle non-finite values.
Results may differ from a plain program's by a relative error of at most 0.0053.
Values may be sent and summed in bfloat16 or wider, within the bound.
No kernel may reach another device: no remote copies, remote signals or barrier semaphores. Data moves between devices by JAX's collectives and lax.ppermute only.
A program may use at most 256 MiB of HBM per device.

v0:
```python
import jax
import jax.numpy as jnp
from jax import lax
from jax.sharding import PartitionSpec as P


def shifted(value, axis, by):
    length = lax.axis_size(axis)
    pairs = [(i, i + by) for i in range(length) if 0 <= i + by < length]
    return lax.ppermute(value, axis, pairs)


def with_halo(value, sides, width):
    for axis, dim in sides:
        size, length = (lax.axis_size(axis), value.shape[dim])
        up = [(i, (i + 1) % size) for i in range(size - 1)]
        down = [(j, i) for i, j in up]
        last = lax.slice_in_dim(value, length - width, length, axis=dim)
        initial = lax.slice_in_dim(value, 0, width, axis=dim)
        before = lax.ppermute(last, axis, up)
        after = lax.ppermute(initial, axis, down)
        value = jnp.concatenate([before, value, after], axis=dim)
    return value


def tap_block(padded, tap_t, tap_h, tap_w, depth_count, row_count, col_count):
    block = padded[
        tap_t : tap_t + depth_count, tap_h : tap_h + row_count, tap_w : tap_w + col_count
    ]
    return block.reshape(-1, block.shape[-1])


def body(frames, cache_in, kernel, conv_bias, cotangent):
    frame_count, row_count, col_count, channels = frames.shape
    is_first = lax.axis_index("tm") == 0
    earlier = shifted(frames, "tm", 1)
    earlier = jnp.where(is_first, cache_in, earlier)
    stacked = jnp.concatenate([earlier, frames], 0)
    extended = with_halo(stacked, (("height", 1), ("width", 2)), 1)
    pre_act = jnp.zeros((frame_count * row_count * col_count, channels), jnp.float32) + conv_bias
    for tap_t in range(3):
        for tap_h in range(3):
            for tap_w in range(3):
                block = tap_block(extended, tap_t, tap_h, tap_w, frame_count, row_count, col_count)
                pre_act = pre_act + lax.dot_general(
                    block,
                    kernel[:, tap_t, tap_h, tap_w, :],
                    (((1,), (1,)), ((), ())),
                    preferred_element_type=jnp.float32,
                )
    sigma = jax.nn.sigmoid(pre_act)
    decoded = (pre_act * sigma).astype(jnp.bfloat16).reshape(frames.shape)
    scaled = (
        cotangent.reshape(-1, channels).astype(jnp.float32)
        * sigma
        * (1.0 + pre_act * (1.0 - sigma))
    ).astype(jnp.bfloat16)
    grad_rimmed = with_halo(scaled.reshape(frames.shape), (("height", 1), ("width", 2)), 1)
    partial_value = jnp.zeros((frame_count + 2, row_count, col_count, channels), jnp.float32)
    for tap_t in range(3):
        contrib = jnp.zeros((frame_count * row_count * col_count, channels), jnp.float32)
        for tap_h in range(3):
            for tap_w in range(3):
                block = grad_rimmed[
                    :, 2 - tap_h : 2 - tap_h + row_count, 2 - tap_w : 2 - tap_w + col_count
                ].reshape(-1, channels)
                contrib = contrib + jnp.dot(
                    block, kernel[:, tap_t, tap_h, tap_w, :], preferred_element_type=jnp.float32
                )
        partial_value = partial_value.at[tap_t : tap_t + frame_count].add(
            contrib.reshape(frame_count, row_count, col_count, channels)
        )
    cache_grad = partial_value[:2].astype(jnp.bfloat16)
    carried = shifted(cache_grad, "tm", -1)
    frame_grad = (
        partial_value[2:]
        .at[frame_count - 2 :]
        .add(carried.astype(jnp.float32))
        .astype(jnp.bfloat16)
    )
    pieces = []
    for tap_t in range(3):
        for tap_h in range(3):
            for tap_w in range(3):
                block = tap_block(extended, tap_t, tap_h, tap_w, frame_count, row_count, col_count)
                pieces.append(
                    lax.dot_general(
                        scaled, block, (((0,), (0,)), ((), ())), preferred_element_type=jnp.float32
                    )
                )
    owned = lax.psum_scatter(
        jnp.stack(pieces, 1).reshape(
            channels // lax.axis_size("height") * lax.axis_size("height"), 3, 3, 3, channels
        ),
        "height",
        scatter_dimension=0,
        tiled=True,
    )
    kernel_grad = lax.psum(owned, ("tm", "width"))
    return (decoded, frame_grad, cache_grad, kernel_grad)


def solution(mesh):
    in_specs = (
        P("tm", "height", "width", None),
        P(None, "height", "width", None),
        P(),
        P(),
        P("tm", "height", "width", None),
    )
    out_specs = (
        P("tm", "height", "width", None),
        P("tm", "height", "width", None),
        P("tm", "height", "width", None),
        P("height", None, None, None, None),
    )
    return jax.shard_map(body, mesh=mesh, in_specs=in_specs, out_specs=out_specs, check_vma=False)
```

profile of v0, /device:TPU:1, one launch (start us, length us, event | category | flops | bytes accessed | tf_op | source)
XLA Modules:
  0.0 323.4 jit_solution(16105572426888722058)
XLA Ops:
  7.2 10.2 %collective-permute-start = (bf16[2,4,32,384]{3,2,1,0:T(8,128)(2,1)}, bf16[2,4,32,384]{3,2,1,0:T(8,128)(2,1)S(1)}, u32[]{:S(2)}, u32[]{:S(2)}) collective-permute-start(bf16[2,4,32,384]{3,2,1,0:T(8,128)(2,1)} %param.15), channel_id=1, source_target_pairs={{0,64},{64,128},{128,192},{1,65},{65,129},{129,193},{2,66},{66,130... | collective-permute-start | bytes 589832 | tf_op jit(solution)/shard_map/ppermute | solution.py:10
  17.4 2.9 collective-permute-done
  21.2 3.2 collective-permute-start.1
  24.4 1.3 collective-permute-start.2
  26.7 3.1 collective-permute-done.2
  30.7 4.8 %collective-permute-start.3 = (bf16[4,6,1,384]{3,2,1,0:T(2,128)(2,1)S(1)}, bf16[4,6,1,384]{3,2,1,0:T(2,128)(2,1)S(1)}, u32[]{:S(2)}, u32[]{:S(2)}) collective-permute-start(bf16[4,6,1,384]{3,2,1,0:T(2,128)(2,1)S(1)} %get-tuple-element.80), channel_id=1, source_target_pairs={{0,1},{1,2},{2,3},{4,5},{5,6},{6,7},{8,9},{9,10},{10,11},{12,13},{... | collective-permute-start | bytes 55304 | tf_op jit(solution)/shard_map/ppermute | solution.py:20
  35.5 1.3 collective-permute-start.4
  36.8 1.1 pad_maximum_fusion.1
  38.1 2.1 collective-permute-done.4
  40.2 1.4 maximum_maximum_fusion
  65.4 1.2 fusion.13
  66.6 1.2 fusion.12
  74.4 1.2 fusion.5
  81.3 3.5 %collective-permute-start.5 = (bf16[2,1,32,384]{3,2,1,0:T(8,128)(2,1)S(1)}, bf16[2,1,32,384]{3,2,1,0:T(8,128)(2,1)S(1)}, u32[]{:S(2)}, u32[]{:S(2)}) collective-permute-start(bf16[2,1,32,384]{3,2,1,0:T(8,128)(2,1)S(1)} %get-tuple-element.106), channel_id=1, source_target_pairs={{0,4},{4,8},{8,12},{12,16},{16,20},{20,24},{24,28},{28,32},{32,36}... | collective-permute-start | bytes 147464 | tf_op jit(solution)/shard_map/ppermute | solution.py:20
  84.7 1.3 collective-permute-start.6
  86.1 3.5 %collective-permute-done.6 = bf16[2,1,32,384]{3,2,1,0:T(8,128)(2,1)S(1)} collective-permute-done((bf16[2,1,32,384]{3,2,1,0:T(8,128)(2,1)S(1)}, bf16[2,1,32,384]{3,2,1,0:T(8,128)(2,1)S(1)}, u32[]{:S(2)}, u32[]{:S(2)}) %collective-permute-start.6) | collective-permute-done | bytes 49184 | tf_op jit(solution)/shard_map/ppermute | solution.py:21
  89.6 1.3 collective-permute-start.7
  90.9 4.2 %collective-permute-start.8 = (bf16[2,6,1,384]{3,2,1,0:T(2,128)(2,1)S(1)}, bf16[2,6,1,384]{3,2,1,0:T(2,128)(2,1)S(1)}, u32[]{:S(2)}, u32[]{:S(2)}) collective-permute-start(bf16[2,6,1,384]{3,2,1,0:T(2,128)(2,1)S(1)} %get-tuple-element.103), channel_id=1, source_target_pairs={{0,1},{1,2},{2,3},{4,5},{5,6},{6,7},{8,9},{9,10},{10,11},{12,13},{... | collective-permute-start | bytes 27656 | tf_op jit(solution)/shard_map/ppermute | solution.py:20
  95.1 1.2 fusion.70
  96.4 1.2 fusion.91
  97.6 1.2 fusion.50
  99.2 1.5 fusion.75
  100.7 1.3 convolution_add_fusion.20
  102.0 1.2 convolution_add_fusion.19
  103.3 1.2 convolution_add_fusion.18
  104.5 1.2 convolution_add_fusion.17
  105.8 1.2 convolution_add_fusion.16
  110.0 1.9 collective-permute-start.9
  113.9 87.3 %reduce-scatter.2.cloned.1.call-done = f32[24,3,3,3,384]{4,0,3,2,1:T(8,128)} async-done(((f32[384,3,3,3,384]{4,0,3,2,1:T(8,128)}), f32[24,3,3,3,384]{4,0,3,2,1:T(8,128)}) %reduce-scatter.2.cloned.1.call-update) | async-done | bytes 995344 | tf_op jit(solution)/shard_map/reduce_scatter | solution.py:91
  201.2 1.2 fusion.30
  203.2 111.2 %all-reduce.3.cloned.1.call-done = f32[24,3,3,3,384]{4,0,3,2,1:T(8,128)} async-done(((f32[24,3,3,3,384]{4,0,3,2,1:T(8,128)}), f32[24,3,3,3,384]{4,0,3,2,1:T(8,128)}) %all-reduce.3.cloned.1.call-update) | async-done | bytes 995344 | tf_op jit(solution)/shard_map/psum | solution.py:99
  314.3 2.2 copy.37
  (112 shorter events, 44.7 us)
Async XLA Ops:
  7.2 194.0 %reduce-scatter.2.cloned.1.call-start = ((), (), s32[]{:S(2)}) async-start(), calls=%async_computation.1 | async-start | bytes 16920576 | tf_op jit(solution)/shard_map/reduce_scatter | solution.py:91
  7.2 13.1 %collective-permute-start = (bf16[2,4,32,384]{3,2,1,0:T(8,128)(2,1)}, bf16[2,4,32,384]{3,2,1,0:T(8,128)(2,1)S(1)}, u32[]{:S(2)}, u32[]{:S(2)}) collective-permute-start(bf16[2,4,32,384]{3,2,1,0:T(8,128)(2,1)} %param.15), channel_id=1, source_target_pairs={{0,64},{64,128},{128,192},{1,65},{65,129},{129,193},{2,66},{66,130... | collective-permute-start | bytes 589832 | tf_op jit(solution)/shard_map/ppermute | solution.py:10
  17.4 24.6 %slice-start = ((s8[7962624]{0:T(1024)(128)(4,1)}), s8[4194304]{0:T(1024)(128)(4,1)S(1)}, s32[]{:S(2)}) async-start(s8[7962624]{0:T(1024)(128)(4,1)} %bitcast.401), calls=%async_computation.3 | async-start | bytes 8388608
  20.4 22.0 %copy-start.2 = (f32[384]{0:T(512)S(1)}, f32[384]{0:T(512)}, u32[]{:S(2)}) copy-start(f32[384]{0:T(512)} %param.18) | copy-start | bytes 4612
  21.2 5.4 %collective-permute-start.1 = (bf16[4,1,32,384]{3,2,1,0:T(8,128)(2,1)S(1)}, bf16[4,1,32,384]{3,2,1,0:T(8,128)(2,1)S(1)}, u32[]{:S(2)}, u32[]{:S(2)}) collective-permute-start(bf16[4,1,32,384]{3,2,1,0:T(8,128)(2,1)S(1)} %get-tuple-element.92), channel_id=1, source_target_pairs={{0,4},{4,8},{8,12},{12,16},{16,20},{20,24},{24,28},{28,32},{32,36}... | collective-permute-start | bytes 294920 | tf_op jit(solution)/shard_map/ppermute | solution.py:20
  24.4 5.4 %collective-permute-start.2 = (bf16[4,1,32,384]{3,2,1,0:T(8,128)(2,1)S(1)}, bf16[4,1,32,384]{3,2,1,0:T(8,128)(2,1)S(1)}, u32[]{:S(2)}, u32[]{:S(2)}) collective-permute-start(bf16[4,1,32,384]{3,2,1,0:T(8,128)(2,1)S(1)} %get-tuple-element.93), channel_id=1, source_target_pairs={{4,0},{8,4},{12,8},{16,12},{20,16},{24,20},{28,24},{32,28},{36,32}... | collective-permute-start | bytes 294920 | tf_op jit(solution)/shard_map/ppermute | solution.py:21
  30.7 7.4 %collective-permute-start.3 = (bf16[4,6,1,384]{3,2,1,0:T(2,128)(2,1)S(1)}, bf16[4,6,1,384]{3,2,1,0:T(2,128)(2,1)S(1)}, u32[]{:S(2)}, u32[]{:S(2)}) collective-permute-start(bf16[4,6,1,384]{3,2,1,0:T(2,128)(2,1)S(1)} %get-tuple-element.80), channel_id=1, source_target_pairs={{0,1},{1,2},{2,3},{4,5},{5,6},{6,7},{8,9},{9,10},{10,11},{12,13},{... | collective-permute-start | bytes 55304 | tf_op jit(solution)/shard_map/ppermute | solution.py:20
  35.5 4.7 %collective-permute-start.4 = (bf16[4,6,1,384]{3,2,1,0:T(2,128)(2,1)S(1)}, bf16[4,6,1,384]{3,2,1,0:T(2,128)(2,1)S(1)}, u32[]{:S(2)}, u32[]{:S(2)}) collective-permute-start(bf16[4,6,1,384]{3,2,1,0:T(2,128)(2,1)S(1)} %get-tuple-element.81), channel_id=1, source_target_pairs={{1,0},{2,1},{3,2},{5,4},{6,5},{7,6},{9,8},{10,9},{11,10},{13,12},{... | collective-permute-start | bytes 55304 | tf_op jit(solution)/shard_map/ppermute | solution.py:21
  38.1 4.0 %slice-start.1 = ((s8[7962624]{0:T(1024)(128)(4,1)}), s8[3768320]{0:T(1024)(128)(4,1)S(1)}, s32[]{:S(2)}) async-start(s8[7962624]{0:T(1024)(128)(4,1)} %bitcast.401), calls=%async_computation.4 | async-start | bytes 7536640
  45.0 3.6 %copy-start = (bf16[2,4,32,384]{3,2,1,0:T(8,128)(2,1)S(1)}, bf16[2,4,32,384]{3,2,1,0:T(8,128)(2,1)}, u32[]{:S(2)}) copy-start(bf16[2,4,32,384]{3,2,1,0:T(8,128)(2,1)} %param.15) | copy-start | bytes 589828
  46.2 3.6 %copy-start.3 = (bf16[2,4,32,384]{3,2,1,0:T(8,128)(2,1)S(1)}, bf16[2,4,32,384]{3,2,1,0:T(8,128)(2,1)}, u32[]{:S(2)}) copy-start(bf16[2,4,32,384]{3,2,1,0:T(8,128)(2,1)} %param.19) | copy-start | bytes 589828
  81.2 233.1 %all-reduce.3.cloned.1.call-start = ((), (), s32[]{:S(2)}) async-start(), calls=%async_computation.2 | async-start | bytes 1990656 | tf_op jit(solution)/shard_map/psum | solution.py:99
  81.2 25.8 %slice-start.2 = ((s8[7962624]{0:T(1024)(128)(4,1)}), s8[3768320]{0:T(1024)(128)(4,1)S(1)}, s32[]{:S(2)}) async-start(s8[7962624]{0:T(1024)(128)(4,1)} %bitcast.403), calls=%async_computation.5 | async-start | bytes 7536640
  81.3 4.8 %collective-permute-start.5 = (bf16[2,1,32,384]{3,2,1,0:T(8,128)(2,1)S(1)}, bf16[2,1,32,384]{3,2,1,0:T(8,128)(2,1)S(1)}, u32[]{:S(2)}, u32[]{:S(2)}) collective-permute-start(bf16[2,1,32,384]{3,2,1,0:T(8,128)(2,1)S(1)} %get-tuple-element.106), channel_id=1, source_target_pairs={{0,4},{4,8},{8,12},{12,16},{16,20},{20,24},{24,28},{28,32},{32,36}... | collective-permute-start | bytes 147464 | tf_op jit(solution)/shard_map/ppermute | solution.py:20
  84.7 4.8 %collective-permute-start.6 = (bf16[2,1,32,384]{3,2,1,0:T(8,128)(2,1)S(1)}, bf16[2,1,32,384]{3,2,1,0:T(8,128)(2,1)S(1)}, u32[]{:S(2)}, u32[]{:S(2)}) collective-permute-start(bf16[2,1,32,384]{3,2,1,0:T(8,128)(2,1)S(1)} %get-tuple-element.107), channel_id=1, source_target_pairs={{4,0},{8,4},{12,8},{16,12},{20,16},{24,20},{28,24},{32,28},{36,32}... | collective-permute-start | bytes 147464 | tf_op jit(solution)/shard_map/ppermute | solution.py:21
  89.6 9.2 %collective-permute-start.7 = (bf16[2,6,1,384]{3,2,1,0:T(2,128)(2,1)S(1)}, bf16[2,6,1,384]{3,2,1,0:T(2,128)(2,1)S(1)}, u32[]{:S(2)}, u32[]{:S(2)}) collective-permute-start(bf16[2,6,1,384]{3,2,1,0:T(2,128)(2,1)S(1)} %get-tuple-element.102), channel_id=1, source_target_pairs={{1,0},{2,1},{3,2},{5,4},{6,5},{7,6},{9,8},{10,9},{11,10},{13,12},{... | collective-permute-start | bytes 27656 | tf_op jit(solution)/shard_map/ppermute | solution.py:21
  90.9 7.9 %collective-permute-start.8 = (bf16[2,6,1,384]{3,2,1,0:T(2,128)(2,1)S(1)}, bf16[2,6,1,384]{3,2,1,0:T(2,128)(2,1)S(1)}, u32[]{:S(2)}, u32[]{:S(2)}) collective-permute-start(bf16[2,6,1,384]{3,2,1,0:T(2,128)(2,1)S(1)} %get-tuple-element.103), channel_id=1, source_target_pairs={{0,1},{1,2},{2,3},{4,5},{5,6},{6,7},{8,9},{9,10},{10,11},{12,13},{... | collective-permute-start | bytes 27656 | tf_op jit(solution)/shard_map/ppermute | solution.py:20
  99.1 7.9 %slice-start.3 = ((s8[7962624]{0:T(1024)(128)(4,1)}), s8[4194304]{0:T(1024)(128)(4,1)S(1)}, s32[]{:S(2)}) async-start(s8[7962624]{0:T(1024)(128)(4,1)} %bitcast.403), calls=%async_computation.6 | async-start | bytes 8388608
  110.0 206.6 %copy-start.1 = (bf16[2,4,32,384]{3,2,1,0:T(8,128)(2,1)}, bf16[2,4,32,384]{3,2,1,0:T(8,128)(2,1)S(1)}, u32[]{:S(2)}) copy-start(bf16[2,4,32,384]{3,2,1,0:T(8,128)(2,1)S(1)} %slice.745) | copy-start | bytes 589828
  110.0 92.4 %collective-permute-start.9 = (bf16[2,4,32,384]{3,2,1,0:T(8,128)(2,1)S(1)}, bf16[2,4,32,384]{3,2,1,0:T(8,128)(2,1)S(1)}, u32[]{:S(2)}, u32[]{:S(2)}) collective-permute-start(bf16[2,4,32,384]{3,2,1,0:T(8,128)(2,1)S(1)} %slice.745), channel_id=1, source_target_pairs={{64,0},{128,64},{192,128},{65,1},{129,65},{193,129},{66,2},{130,66... | collective-permute-start | bytes 589832 | tf_op jit(solution)/shard_map/ppermute | solution.py:10
Sparse Core Ops, SparseCore 0:
  81.3 119.7 reduce-scatter.1
  203.5 110.8 all-reduce.2
where the time goes:
time: 324 us; the launch traced here: 323 us
  waiting for transfers between devices  210 us (65%)
  matrix products  56 us (17%)
  starting transfers between devices  33 us (10%)
  between operations  14.8 us (5%)
  other arithmetic  6.37 us (2%)
    psum x1, waiting for transfers between devices, body(): kernel_grad = lax.psum(owned, ('tm', 'width'))  111 us
    reduce_scatter x1, waiting for transfers between devices, body(): lax.psum_scatter(jnp.stack(pieces, 1).reshape(channels // lax.axis_size('...  87.3 us
    dot_general x27, matrix products, body(): lax.dot_general(scaled, block, (((0,), (0,)), ((), ())), preferred_elemen...  30.3 us
    dot_general x27, matrix products, body(): jnp.dot(block, kernel[:, tap_t, tap_h, tap_w, :], preferred_element_type=...  17.2 us
    ppermute x4, starting transfers between devices, with_halo(): before = lax.ppermute(last, axis, up)  15.6 us
    ppermute x2, starting transfers between devices, shifted(): return lax.ppermute(value, axis, pairs)  12.1 us
    ppermute x4, waiting for transfers between devices, with_halo(): after = lax.ppermute(initial, axis, down)  8.73 us
    dot_general x27, matrix products, body(): lax.dot_general(block, kernel[:, tap_t, tap_h, tap_w, :], (((1,), (1,)),...  8.56 us
  transfers between devices with their start and end apart: 12, of which 6 were waited for; matrix products, arithmetic and copies ran while one was open for 6% of the time, Pallas kernels for 0%

commit v1 on v0

--- a/solution.py
+++ b/solution.py
@@ -2,6 +2,7 @@
 import jax.numpy as jnp
 from jax import lax
 from jax.sharding import PartitionSpec as P
+from jax.lax import all_gather
 
 
 def shifted(value, axis, by):
@@ -96,7 +97,8 @@
         scatter_dimension=0,
         tiled=True,
     )
-    kernel_grad = lax.psum(owned, ("tm", "width"))
+    v1 = all_gather(owned, ("tm", "width"))
+    kernel_grad = jnp.sum(v1, axis=0)
     return (decoded, frame_grad, cache_grad, kernel_grad)
 
 

time: 324 us -> 475 us (1.47)
  waiting for transfers between devices: 210 us -> 354 us
  other arithmetic: 6.37 us -> 13.7 us
    all_gather x0 -> x1, waiting for transfers between devices: none -> 211 us  [body(): v1 = all_gather(owned, ('tm', 'width'))]
    psum x1 -> x0, waiting for transfers between devices: 111 us -> none  [body(): kernel_grad = lax.psum(owned, ('tm', 'width'))]
    reduce_scatter x1, waiting for transfers between devices: 87.3 us -> 120 us  [body(): lax.psum_scatter(jnp.stack(pieces, 1).reshape(channels // lax.axis_size('...]
    ppermute x2, waiting for transfers between devices: 2.89 us -> 13.7 us  [shifted(): return lax.ppermute(value, axis, pairs)]
    reduce_sum x0 -> x1, other arithmetic: none -> 7.36 us  [body(): kernel_grad = jnp.sum(v1, axis=0)]
  transfers between devices with their start and end apart: 12 -> 12, of which waited for: 6 -> 7; matrix products, arithmetic and copies ran while one was open for 6% -> 4% of each run, Pallas kernels for 0% -> 0%
where the time goes in v1:
time: 475 us; the launch traced here: 474 us
  waiting for transfers between devices  354 us (75%)
  matrix products  55.9 us (12%)
  starting transfers between devices  34.8 us (7%)
  between operations  14.8 us (3%)
  other arithmetic  13.7 us (3%)
    all_gather x1, waiting for transfers between devices, body(): v1 = all_gather(owned, ('tm', 'width'))  211 us
    reduce_scatter x1, waiting for transfers between devices, body(): lax.psum_scatter(jnp.stack(pieces, 1).reshape(channels // lax.axis_size('...  120 us
    dot_general x27, matrix products, body(): lax.dot_general(scaled, block, (((0,), (0,)), ((), ())), preferred_elemen...  30.3 us
    dot_general x27, matrix products, body(): jnp.dot(block, kernel[:, tap_t, tap_h, tap_w, :], preferred_element_type=...  17.1 us
    ppermute x2, starting transfers between devices, shifted(): return lax.ppermute(value, axis, pairs)  15.2 us
    ppermute x4, starting transfers between devices, with_halo(): before = lax.ppermute(last, axis, up)  14.4 us
    ppermute x2, waiting for transfers between devices, shifted(): return lax.ppermute(value, axis, pairs)  13.7 us
  transfers between devices with their start and end apart: 12, of which 7 were waited for; matrix products, arithmetic and copies ran while one was open for 4% of the time, Pallas kernels for 0%

profile of v1, /device:TPU:1, one launch (start us, length us, event | category | flops | bytes accessed | tf_op | source)
XLA Modules:
  0.0 473.8 jit_solution(3823915267147225844)
XLA Ops:
  7.2 10.2 %collective-permute-start = (bf16[2,4,32,384]{3,2,1,0:T(8,128)(2,1)}, bf16[2,4,32,384]{3,2,1,0:T(8,128)(2,1)S(1)}, u32[]{:S(2)}, u32[]{:S(2)}) collective-permute-start(bf16[2,4,32,384]{3,2,1,0:T(8,128)(2,1)} %param.15), channel_id=1, source_target_pairs={{0,64},{64,128},{128,192},{1,65},{65,129},{129,193},{2,66},{66,130... | collective-permute-start | bytes 589832 | tf_op jit(solution)/shard_map/ppermute | solution.py:11
  17.4 2.9 collective-permute-done
  21.2 3.2 collective-permute-start.1
  24.4 1.3 collective-permute-start.2
  26.7 3.1 collective-permute-done.2
  30.7 4.8 %collective-permute-start.3 = (bf16[4,6,1,384]{3,2,1,0:T(2,128)(2,1)S(1)}, bf16[4,6,1,384]{3,2,1,0:T(2,128)(2,1)S(1)}, u32[]{:S(2)}, u32[]{:S(2)}) collective-permute-start(bf16[4,6,1,384]{3,2,1,0:T(2,128)(2,1)S(1)} %get-tuple-element.80), channel_id=1, source_target_pairs={{0,1},{1,2},{2,3},{4,5},{5,6},{6,7},{8,9},{9,10},{10,11},{12,13},{... | collective-permute-start | bytes 55304 | tf_op jit(solution)/shard_map/ppermute | solution.py:21
  35.5 1.3 collective-permute-start.4
  38.1 2.1 collective-permute-done.4
  40.2 1.4 maximum_maximum_fusion
  65.4 1.2 fusion.13
  66.6 1.2 fusion.12
  74.4 1.2 fusion.5
  81.2 119.9 %reduce-scatter.2.cloned.1.call-done = f32[24,3,3,3,384]{4,0,3,2,1:T(8,128)} async-done(((f32[384,3,3,3,384]{4,0,3,2,1:T(8,128)}), f32[24,3,3,3,384]{4,0,3,2,1:T(8,128)}) %reduce-scatter.2.cloned.1.call-update) | async-done | bytes 995344 | tf_op jit(solution)/shard_map/reduce_scatter | solution.py:92
  201.2 2.5 collective-permute-start.5
  203.7 1.3 collective-permute-start.6
  205.0 3.6 collective-permute-done.6
  208.7 1.3 collective-permute-start.7
  210.0 4.0 collective-permute-start.8
  214.0 1.3 fusion.70
  215.3 1.2 fusion.91
  216.5 1.2 fusion.50
  218.2 1.4 fusion.75
  219.5 1.2 convolution_add_fusion.20
  220.8 1.2 convolution_add_fusion.19
  222.0 1.2 convolution_add_fusion.18
  223.3 1.2 convolution_add_fusion.17
  224.5 1.2 convolution_add_fusion.16
  225.8 1.2 convolution_add_fusion.15
  229.7 5.0 %collective-permute-start.9 = (bf16[2,4,32,384]{3,2,1,0:T(8,128)(2,1)S(1)}, bf16[2,4,32,384]{3,2,1,0:T(8,128)(2,1)S(1)}, u32[]{:S(2)}, u32[]{:S(2)}) collective-permute-start(bf16[2,4,32,384]{3,2,1,0:T(8,128)(2,1)S(1)} %slice.745), channel_id=1, source_target_pairs={{64,0},{128,64},{192,128},{65,1},{129,65},{193,129},{66,2},{130,66... | collective-permute-start | bytes 589832 | tf_op jit(solution)/shard_map/ppermute | solution.py:11
  236.9 10.8 %collective-permute-done.9 = bf16[2,4,32,384]{3,2,1,0:T(8,128)(2,1)S(1)} collective-permute-done((bf16[2,4,32,384]{3,2,1,0:T(8,128)(2,1)S(1)}, bf16[2,4,32,384]{3,2,1,0:T(8,128)(2,1)S(1)}, u32[]{:S(2)}, u32[]{:S(2)}) %collective-permute-start.9) | collective-permute-done | bytes 196640 | tf_op jit(solution)/shard_map/ppermute | solution.py:11
  248.5 211.2 %all-gather.3.cloned.1.call-done = f32[384,3,3,3,384]{4,0,3,2,1:T(8,128)} async-done(((f32[24,3,3,3,384]{4,0,3,2,1:T(8,128)}), f32[384,3,3,3,384]{4,0,3,2,1:T(8,128)}) %all-gather.3.cloned.1.call-update) | async-done | bytes 15925264 | tf_op jit(solution)/shard_map/all_gather | solution.py:100
  459.6 7.4 %reduce_sum.9 = f32[24,3,3,3,384]{4,0,3,2,1:T(8,128)} reduce(f32[16,24,3,3,3,384]{5,1,0,4,3,2:T(8,128)} %bitcast.406, f32[]{:T(128)} %constant.126.clone.1), dimensions={0}, to_apply=%region_1.2 | reduce | flops 3732480 | bytes 16920580 | tf_op jit(solution)/shard_map/reduce_sum | solution.py:101
  (112 shorter events, 45.8 us)
Async XLA Ops:
  7.2 194.0 %reduce-scatter.2.cloned.1.call-start = ((), (), s32[]{:S(2)}) async-start(), calls=%async_computation.1 | async-start | bytes 16920576 | tf_op jit(solution)/shard_map/reduce_scatter | solution.py:92
  7.2 13.1 %collective-permute-start = (bf16[2,4,32,384]{3,2,1,0:T(8,128)(2,1)}, bf16[2,4,32,384]{3,2,1,0:T(8,128)(2,1)S(1)}, u32[]{:S(2)}, u32[]{:S(2)}) collective-permute-start(bf16[2,4,32,384]{3,2,1,0:T(8,128)(2,1)} %param.15), channel_id=1, source_target_pairs={{0,64},{64,128},{128,192},{1,65},{65,129},{129,193},{2,66},{66,130... | collective-permute-start | bytes 589832 | tf_op jit(solution)/shard_map/ppermute | solution.py:11
  17.4 24.6 %slice-start = ((s8[7962624]{0:T(1024)(128)(4,1)}), s8[4194304]{0:T(1024)(128)(4,1)S(1)}, s32[]{:S(2)}) async-start(s8[7962624]{0:T(1024)(128)(4,1)} %bitcast.402), calls=%async_computation.3 | async-start | bytes 8388608
  20.4 22.0 %copy-start.2 = (f32[384]{0:T(512)S(1)}, f32[384]{0:T(512)}, u32[]{:S(2)}) copy-start(f32[384]{0:T(512)} %param.18) | copy-start | bytes 4612
  21.2 5.4 %collective-permute-start.1 = (bf16[4,1,32,384]{3,2,1,0:T(8,128)(2,1)S(1)}, bf16[4,1,32,384]{3,2,1,0:T(8,128)(2,1)S(1)}, u32[]{:S(2)}, u32[]{:S(2)}) collective-permute-start(bf16[4,1,32,384]{3,2,1,0:T(8,128)(2,1)S(1)} %get-tuple-element.92), channel_id=1, source_target_pairs={{0,4},{4,8},{8,12},{12,16},{16,20},{20,24},{24,28},{28,32},{32,36}... | collective-permute-start | bytes 294920 | tf_op jit(solution)/shard_map/ppermute | solution.py:21
  24.4 5.4 %collective-permute-start.2 = (bf16[4,1,32,384]{3,2,1,0:T(8,128)(2,1)S(1)}, bf16[4,1,32,384]{3,2,1,0:T(8,128)(2,1)S(1)}, u32[]{:S(2)}, u32[]{:S(2)}) collective-permute-start(bf16[4,1,32,384]{3,2,1,0:T(8,128)(2,1)S(1)} %get-tuple-element.93), channel_id=1, source_target_pairs={{4,0},{8,4},{12,8},{16,12},{20,16},{24,20},{28,24},{32,28},{36,32}... | collective-permute-start | bytes 294920 | tf_op jit(solution)/shard_map/ppermute | solution.py:22
  30.7 7.4 %collective-permute-start.3 = (bf16[4,6,1,384]{3,2,1,0:T(2,128)(2,1)S(1)}, bf16[4,6,1,384]{3,2,1,0:T(2,128)(2,1)S(1)}, u32[]{:S(2)}, u32[]{:S(2)}) collective-permute-start(bf16[4,6,1,384]{3,2,1,0:T(2,128)(2,1)S(1)} %get-tuple-element.80), channel_id=1, source_target_pairs={{0,1},{1,2},{2,3},{4,5},{5,6},{6,7},{8,9},{9,10},{10,11},{12,13},{... | collective-permute-start | bytes 55304 | tf_op jit(solution)/shard_map/ppermute | solution.py:21
  35.5 4.7 collective-permute-start.4
  38.1 4.0 slice-start.1
  45.0 3.6 copy-start
  46.2 3.6 copy-start.3
  81.2 378.5 %all-gather.3.cloned.1.call-start = ((), (), s32[]{:S(2)}) async-start(), calls=%async_computation.2 | async-start | bytes 16920576 | tf_op jit(solution)/shard_map/all_gather | solution.py:100
  201.2 25.8 %slice-start.2 = ((s8[7962624]{0:T(1024)(128)(4,1)}), s8[3768320]{0:T(1024)(128)(4,1)S(1)}, s32[]{:S(2)}) async-start(s8[7962624]{0:T(1024)(128)(4,1)} %bitcast.404), calls=%async_computation.5 | async-start | bytes 7536640
  201.2 3.8 collective-permute-start.5
  203.7 4.9 %collective-permute-start.6 = (bf16[2,1,32,384]{3,2,1,0:T(8,128)(2,1)S(1)}, bf16[2,1,32,384]{3,2,1,0:T(8,128)(2,1)S(1)}, u32[]{:S(2)}, u32[]{:S(2)}) collective-permute-start(bf16[2,1,32,384]{3,2,1,0:T(8,128)(2,1)S(1)} %get-tuple-element.107), channel_id=1, source_target_pairs={{4,0},{8,4},{12,8},{16,12},{20,16},{24,20},{28,24},{32,28},{36,32}... | collective-permute-start | bytes 147464 | tf_op jit(solution)/shard_map/ppermute | solution.py:22
  208.7 9.1 %collective-permute-start.7 = (bf16[2,6,1,384]{3,2,1,0:T(2,128)(2,1)S(1)}, bf16[2,6,1,384]{3,2,1,0:T(2,128)(2,1)S(1)}, u32[]{:S(2)}, u32[]{:S(2)}) collective-permute-start(bf16[2,6,1,384]{3,2,1,0:T(2,128)(2,1)S(1)} %get-tuple-element.102), channel_id=1, source_target_pairs={{1,0},{2,1},{3,2},{5,4},{6,5},{7,6},{9,8},{10,9},{11,10},{13,12},{... | collective-permute-start | bytes 27656 | tf_op jit(solution)/shard_map/ppermute | solution.py:22
  210.0 7.8 %collective-permute-start.8 = (bf16[2,6,1,384]{3,2,1,0:T(2,128)(2,1)S(1)}, bf16[2,6,1,384]{3,2,1,0:T(2,128)(2,1)S(1)}, u32[]{:S(2)}, u32[]{:S(2)}) collective-permute-start(bf16[2,6,1,384]{3,2,1,0:T(2,128)(2,1)S(1)} %get-tuple-element.103), channel_id=1, source_target_pairs={{0,1},{1,2},{2,3},{4,5},{5,6},{6,7},{8,9},{9,10},{10,11},{12,13},{... | collective-permute-start | bytes 27656 | tf_op jit(solution)/shard_map/ppermute | solution.py:21
  218.1 8.9 %slice-start.3 = ((s8[7962624]{0:T(1024)(128)(4,1)}), s8[4194304]{0:T(1024)(128)(4,1)S(1)}, s32[]{:S(2)}) async-start(s8[7962624]{0:T(1024)(128)(4,1)} %bitcast.404), calls=%async_computation.6 | async-start | bytes 8388608
  229.7 237.3 %copy-start.1 = (bf16[2,4,32,384]{3,2,1,0:T(8,128)(2,1)}, bf16[2,4,32,384]{3,2,1,0:T(8,128)(2,1)S(1)}, u32[]{:S(2)}) copy-start(bf16[2,4,32,384]{3,2,1,0:T(8,128)(2,1)S(1)} %slice.745) | copy-start | bytes 589828
  229.7 18.0 %collective-permute-start.9 = (bf16[2,4,32,384]{3,2,1,0:T(8,128)(2,1)S(1)}, bf16[2,4,32,384]{3,2,1,0:T(8,128)(2,1)S(1)}, u32[]{:S(2)}, u32[]{:S(2)}) collective-permute-start(bf16[2,4,32,384]{3,2,1,0:T(8,128)(2,1)S(1)} %slice.745), channel_id=1, source_target_pairs={{64,0},{128,64},{192,128},{65,1},{129,65},{193,129},{66,2},{130,66... | collective-permute-start | bytes 589832 | tf_op jit(solution)/shard_map/ppermute | solution.py:11
Sparse Core Ops, SparseCore 0:
  81.3 119.8 reduce-scatter.1
  203.0 256.6 all-gather.2
